TPU v7x, 512 devices: a whole 4x4x16 slice. The times are simulated.
512 devices in a mesh: dp: 16 (over z), pipe: 4 (over x), tensor: 8 (over y, core).
Axes of the slice: x: 4, y: 4, z: 16, core: 2. Of those that a mesh axis runs over, the one named last changes fastest.
Arguments:
- tokens: bfloat16 [16384, 8192], P('dp', ('pipe', 'tensor')), may hold values from -6 to 6
- key_value_weight: bfloat16 [8192, 2048], P(('pipe', 'tensor')), may hold values from -0.0625 to 0.0625
- adapter_down: bfloat16 [96, 8192, 128], P(None, ('pipe', 'tensor', 'dp')), may hold values from -0.0625 to 0.0625
- adapter_up: bfloat16 [96, 64, 2048], P(None, 'dp'), may hold values from -0.75 to 0.75
- tenant_of_block: int32 [128], replicated, may hold values from 0 to 95
- slot_of_tenant: int32 [96], replicated, may hold values from 0 to 95, each once
- cotangent: bfloat16 [16384, 2048], P(('dp', 'pipe', 'tensor')), may hold values from -1.5 to 1.5
Outputs:
- key_value: bfloat16 [16384, 2048], P(('dp', 'pipe', 'tensor'))
- input_grad: bfloat16 [16384, 8192], P('dp', ('pipe', 'tensor'))
- grad_a: float32 [96, 8192, 128], P(None, ('pipe', 'tensor', 'dp'))
- grad_b: float32 [96, 64, 2048], P(None, 'dp', ('pipe', 'tensor'))
Inputs may be any that keep to these rules, and one draw needn't show every extreme that they name: `slot_of_tenant`: each slot holds exactly one tenant.
All inputs are finite; a program needn't handle non-finite values.
Results may differ from a plain program's by a relative error of at most 0.017.
Values may be sent and summed in bfloat16 or wider, within the bound.
A program may use at most 64 MiB of HBM per device.

v0:
```python
import jax
import jax.numpy as jnp
from jax import lax
from jax.sharding import PartitionSpec as P

KEY_WIDTH = 1024
ADAPTER_RANK = 64
BLOCK = 128


def body(
    tokens, key_value_weight, adapter_down, adapter_up, tenant_of_block, slot_of_tenant, cotangent
):
    data_count = lax.axis_size("dp")
    group_count = lax.axis_size(("pipe", "tensor"))
    my_group = lax.axis_index(("pipe", "tensor"))
    tok_dev, feature_count = tokens.shape
    blocks_dev = tok_dev // BLOCK
    row_count = tok_dev // group_count
    tenant_list = slot_of_tenant.shape[0]
    all_blocks = tenant_of_block.shape[0]
    tenant_ids = lax.broadcasted_iota(jnp.int32, (all_blocks, tenant_list), 1)
    slot_of_block = jnp.sum(
        jnp.where(tenant_of_block[:, None] == tenant_ids, slot_of_tenant[None, :], 0), axis=1
    )
    slot_match = slot_of_block[:, None] == tenant_ids
    down_rows = adapter_down.shape[1]
    a_send = jnp.dot(
        slot_match.astype(jnp.bfloat16),
        adapter_down.reshape(tenant_list, down_rows * 2 * ADAPTER_RANK),
        preferred_element_type=jnp.float32,
    )
    a_send = a_send.astype(jnp.bfloat16).reshape(all_blocks, down_rows, 2 * ADAPTER_RANK)
    own_block = my_group * row_count // BLOCK
    own_slots = lax.dynamic_index_in_dim(
        slot_of_block.reshape(data_count, blocks_dev), own_block, 1, False
    )
    owner_choice = (
        own_slots[:, None] == lax.broadcasted_iota(jnp.int32, (data_count, tenant_list), 1)
    ).astype(jnp.bfloat16)
    up_rows = adapter_up.shape[1]
    b_send = jnp.dot(
        owner_choice,
        adapter_up.reshape(tenant_list, up_rows * 2 * KEY_WIDTH),
        preferred_element_type=jnp.float32,
    )
    b_send = b_send.astype(jnp.bfloat16).reshape(data_count, up_rows, 2 * KEY_WIDTH)
    down_blocks, b_own = (
        lax.all_to_all(a_send, "dp", split_axis=0, concat_axis=1, tiled=True),
        lax.all_to_all(b_send, "dp", split_axis=0, concat_axis=1, tiled=True),
    )
    b_own = b_own[0]
    tok_blocks = tokens.reshape(blocks_dev, BLOCK, feature_count)
    low_part = jnp.einsum(
        "bif,bfr->bir", tok_blocks, down_blocks, preferred_element_type=jnp.float32
    ).reshape(tok_dev, 2 * ADAPTER_RANK)
    low_all = lax.psum(low_part.astype(jnp.bfloat16), ("pipe", "tensor"))
    base_out = lax.psum_scatter(
        jnp.dot(tokens, key_value_weight, preferred_element_type=jnp.float32).astype(jnp.bfloat16),
        ("pipe", "tensor"),
        scatter_dimension=0,
        tiled=True,
    ).astype(jnp.float32)
    low_rows = lax.dynamic_slice_in_dim(low_all, my_group * row_count, row_count, 0)
    lowrank = jnp.concatenate(
        [
            jnp.dot(
                low_rows[:, :ADAPTER_RANK], b_own[:, :KEY_WIDTH], preferred_element_type=jnp.float32
            ),
            jnp.dot(
                low_rows[:, ADAPTER_RANK:], b_own[:, KEY_WIDTH:], preferred_element_type=jnp.float32
            ),
        ],
        axis=1,
    )
    key_value = (base_out + lowrank).astype(jnp.bfloat16)
    contract_last = (((1,), (1,)), ((), ()))
    grad_rows = jnp.concatenate(
        [
            lax.dot_general(
                cotangent[:, :KEY_WIDTH],
                b_own[:, :KEY_WIDTH],
                contract_last,
                preferred_element_type=jnp.float32,
            ),
            lax.dot_general(
                cotangent[:, KEY_WIDTH:],
                b_own[:, KEY_WIDTH:],
                contract_last,
                preferred_element_type=jnp.float32,
            ),
        ],
        axis=1,
    )
    grad_rows = grad_rows.astype(jnp.bfloat16)
    cot_all, grad_low = (
        lax.all_gather(cotangent, ("pipe", "tensor"), axis=0, tiled=True),
        lax.all_gather(grad_rows, ("pipe", "tensor"), axis=0, tiled=True),
    )
    grad_blocks = grad_low.reshape(blocks_dev, BLOCK, 2 * ADAPTER_RANK)
    input_grad = lax.dot_general(
        cot_all, key_value_weight, contract_last, preferred_element_type=jnp.float32
    )
    input_grad = input_grad + jnp.einsum(
        "bir,bfr->bif", grad_blocks, down_blocks, preferred_element_type=jnp.float32
    ).reshape(tok_dev, feature_count)
    input_grad = input_grad.astype(jnp.bfloat16)
    grad_a_part = jnp.einsum(
        "bif,bir->bfr", tok_blocks, grad_blocks, preferred_element_type=jnp.float32
    )
    col_count = 2 * KEY_WIDTH // group_count
    col_start = my_group * col_count
    half_index = col_start // KEY_WIDTH
    low_half = lax.dynamic_slice_in_dim(
        low_all, half_index * ADAPTER_RANK, ADAPTER_RANK, 1
    ).reshape(blocks_dev, BLOCK, ADAPTER_RANK)
    cot_cols = lax.dynamic_slice_in_dim(cot_all, col_start, col_count, 1).reshape(
        blocks_dev, BLOCK, col_count
    )
    grad_b_part = jnp.einsum("bir,bic->brc", low_half, cot_cols, preferred_element_type=jnp.float32)
    grad_a_recv, grad_b_recv = (
        lax.all_to_all(
            grad_a_part.astype(jnp.bfloat16), "dp", split_axis=1, concat_axis=0, tiled=True
        ).astype(grad_a_part.dtype),
        lax.all_to_all(
            grad_b_part.astype(jnp.bfloat16), "dp", split_axis=1, concat_axis=0, tiled=True
        ).astype(grad_b_part.dtype),
    )
    slot_weight = slot_match.astype(jnp.float32)
    grad_a = jnp.einsum(
        "bt,bx->tx",
        slot_weight,
        grad_a_recv.reshape(all_blocks, down_rows * 2 * ADAPTER_RANK),
        precision=lax.Precision.HIGHEST,
    )
    grad_a = grad_a.reshape(tenant_list, down_rows, 2 * ADAPTER_RANK)
    grad_b = jnp.einsum(
        "bt,bx->tx",
        slot_weight,
        grad_b_recv.reshape(all_blocks, grad_b_recv.shape[1] * col_count),
        precision=lax.Precision.HIGHEST,
    )
    grad_b = grad_b.reshape(tenant_list, grad_b_recv.shape[1], col_count)
    return (key_value, input_grad, grad_a, grad_b)


def solution(mesh):
    placed = (
        P("dp", ("pipe", "tensor")),
        P(("pipe", "tensor"), None),
        P(None, ("pipe", "tensor", "dp"), None),
        P(None, "dp", None),
        P(),
        P(),
        P(("dp", "pipe", "tensor"), None),
    )
    return jax.shard_map(
        body,
        mesh=mesh,
        in_specs=placed,
        out_specs=(
            P(("dp", "pipe", "tensor"), None),
            P("dp", ("pipe", "tensor")),
            P(None, ("pipe", "tensor", "dp"), None),
            P(None, "dp", ("pipe", "tensor")),
        ),
        check_vma=False,
    )
```

profile of v0, /device:TPU:2, one launch (start us, length us, event | category | flops | bytes accessed | tf_op | source)
XLA Modules:
  0.0 395.1 jit_solution(17106891758424243477)
XLA Ops:
  7.2 0.9 select_reduce_fusion
  8.1 1.3 fusion.2
  9.5 0.1 copy.60
  9.6 44.1 %all_to_all.57 = bf16[128,16,128]{2,1,0:T(8,128)(2,1)S(1)} all-to-all(bf16[128,16,128]{2,1,0:T(8,128)(2,1)S(1)} %bitcast.78), channel_id=1, replica_groups=mesh['dp'=16,'pipe'=4,'tensor'=8] {'dp'}, dimensions={0} | all-to-all | bytes 1048576 | tf_op jit(solution)/shard_map/all_to_all | solution.py:49
  53.7 0.8 copy-done.2
  54.5 0.3 convolution_convert_fusion.4
  54.8 0.9 copy.41
  55.7 0.0 reduce-scatter.2.cloned.1.call-start
  55.7 3.2 convolution_convert_fusion.1
  59.0 0.0 all-gather.2.cloned.1.call-start
  59.1 0.7 all-gather.2.cloned.1.call-update
  59.8 0.1 reshape.62
  59.8 2.4 copy.61
  62.3 0.2 dynamic-slice_reduce_fusion
  62.5 0.4 convolution_convert_fusion
  62.9 0.2 reshape.64
  63.0 24.5 %all_to_all.58 = bf16[16,4,2048]{2,1,0:T(4,128)(2,1)S(1)} all-to-all(bf16[16,4,2048]{2,1,0:T(4,128)(2,1)S(1)} %reshape.64), channel_id=1, replica_groups=mesh['dp'=16,'pipe'=4,'tensor'=8] {'dp'}, dimensions={0} | all-to-all | bytes 524288 | tf_op jit(solution)/shard_map/all_to_all | solution.py:50
  87.5 0.1 squeeze.5
  87.6 0.1 fusion.3
  87.8 0.2 fusion.4
  87.9 0.4 copy-done.4
  88.3 0.1 pad_maximum_fusion
  88.4 24.9 %all_gather.7 = bf16[1024,128]{1,0:T(8,128)(2,1)S(1)} all-gather(bf16[32,128]{1,0:T(8,128)(2,1)S(1)} %pad_maximum_fusion), channel_id=1, replica_groups=mesh['dp'=16,'pipe'=4,'tensor'=8] {'pipe','tensor'}, dimensions={0}, use_global_device_ids=true | all-gather | bytes 270336 | tf_op jit(solution)/shard_map/all_gather | solution.py:98
  113.3 0.3 fusion.1
  113.6 1.1 copy.43
  114.7 5.8 %all-to-all-start.2 = ((bf16[8,256,128]{2,0,1:T(8,128)(2,1)}), bf16[8,256,128]{2,0,1:T(8,128)(2,1)S(1)}, u32[]{:S(2)}, u32[]{:S(2)}) async-start(bf16[8,256,128]{2,0,1:T(8,128)(2,1)} %copy.43), calls=%async_computation.3 | async-start | bytes 1048576 | tf_op jit(solution)/shard_map/all_to_all | solution.py:122
  120.5 0.3 fusion.30
  120.8 63.9 %all-reduce.2.cloned.1.call-done = bf16[1024,128]{0,1:T(8,128)(2,1)} async-done(((bf16[1024,128]{0,1:T(8,128)(2,1)}), bf16[1024,128]{0,1:T(8,128)(2,1)}) %all-reduce.2.cloned.1.call-update) | async-done | bytes 262160 | tf_op jit(solution)/shard_map/psum | solution.py:57
  184.8 1.2 fusion.14
  185.9 1.2 fusion.11
  187.1 0.3 copy.46
  187.4 0.3 fusion.21
  187.7 1.3 copy.53
  189.1 105.7 %reduce-scatter.2.cloned.1.call-done = bf16[32,2048]{1,0:T(8,128)(2,1)} async-done(((bf16[1024,2048]{1,0:T(8,128)(2,1)}), bf16[32,2048]{1,0:T(8,128)(2,1)}) %reduce-scatter.2.cloned.1.call-update) | async-done | bytes 131088 | tf_op jit(solution)/shard_map/reduce_scatter | solution.py:58
  294.8 1.6 fusion.7
  296.4 62.4 %all-gather.2.cloned.1.call-done = bf16[1024,2048]{1,0:T(8,128)(2,1)} async-done(((bf16[32,2048]{1,0:T(8,128)(2,1)}), bf16[1024,2048]{1,0:T(8,128)(2,1)}) %all-gather.2.cloned.1.call-update) | async-done | bytes 4194320 | tf_op jit(solution)/shard_map/all_gather | solution.py:97
  358.8 1.1 constant_dynamic-slice_fusion
  359.9 1.1 convolution_convert_fusion.5
  361.0 0.1 copy.73
  361.1 0.8 reshape.73
  361.9 12.3 %all-to-all-start.3 = ((bf16[16,2,1024]{2,1,0:T(2,128)(2,1)}), bf16[16,2,1024]{2,1,0:T(2,128)(2,1)S(1)}, u32[]{:S(2)}, u32[]{:S(2)}) async-start(bf16[16,2,1024]{2,1,0:T(2,128)(2,1)} %reshape.73), calls=%async_computation.4 | async-start | bytes 131072 | tf_op jit(solution)/shard_map/all_to_all | solution.py:125
  374.2 4.3 %fusion = bf16[1024,256]{1,0:T(8,128)(2,1)} fusion(f32[1024,256]{1,0:T(8,128)S(1)} %bitcast.81, bf16[1024,2048]{1,0:T(8,128)(2,1)} %all-gather.2.cloned.1.call-done, bf16[256,2048]{1,0:T(8,128)(2,1)S(1)} %copy-done), kind=kOutput, calls=%fused_computation.4 | convolution fusion | flops 1074266112 | bytes 6815744 | tf_op jit(solution)/shard_map/dot_general | solution.py:101
  378.4 8.9 %all-to-all-done.3 = bf16[16,2,1024]{2,1,0:T(2,128)(2,1)S(1)} async-done(((bf16[16,2,1024]{2,1,0:T(2,128)(2,1)}), bf16[16,2,1024]{2,1,0:T(2,128)(2,1)S(1)}, u32[]{:S(2)}, u32[]{:S(2)}) %all-to-all-start.3) | async-done | bytes 65568 | tf_op jit(solution)/shard_map/all_to_all | solution.py:125
  387.3 0.1 reshape.74
  387.5 0.1 copy.72
  387.5 0.1 reshape.70
  387.7 0.1 copy.52
  387.8 0.8 fusion.19
  (15 shorter events, 0.1 us)
Async XLA Ops:
  7.2 48.6 %copy-start = (bf16[256,2048]{1,0:T(8,128)(2,1)S(1)}, bf16[256,2048]{1,0:T(8,128)(2,1)}, u32[]{:S(2)}) copy-start(bf16[256,2048]{1,0:T(8,128)(2,1)} %param.8) | copy-start | bytes 3145732
  7.2 47.3 %copy-start.1 = (bf16[1024,256]{1,0:T(8,128)(2,1)S(1)}, bf16[1024,256]{1,0:T(8,128)(2,1)}, u32[]{:S(2)}) copy-start(bf16[1024,256]{1,0:T(8,128)(2,1)} %param.7) | copy-start | bytes 1572868
  7.2 177.6 %all-reduce.2.cloned.1.call-start = ((), (), s32[]{:S(2)}) async-start(), calls=%async_computation.6 | async-start | bytes 524288 | tf_op jit(solution)/shard_map/psum | solution.py:57
  53.7 0.8 copy-start.2
  55.7 239.1 %reduce-scatter.2.cloned.1.call-start = ((), (), s32[]{:S(2)}) async-start(), calls=%async_computation.5 | async-start | bytes 4325376 | tf_op jit(solution)/shard_map/reduce_scatter | solution.py:58
  59.0 28.6 %copy-start.5 = (bf16[32,2048]{1,0:T(8,128)(2,1)S(1)}, bf16[32,2048]{1,0:T(8,128)(2,1)}, u32[]{:S(2)}) copy-start(bf16[32,2048]{1,0:T(8,128)(2,1)} %param.13) | copy-start | bytes 393220
  59.0 299.8 %all-gather.2.cloned.1.call-start = ((), (), s32[]{:S(2)}) async-start(), calls=%async_computation.7 | async-start | bytes 4325376 | tf_op jit(solution)/shard_map/all_gather | solution.py:97
  62.8 57.7 %copy-start.3 = (bf16[16,8,16,128]{3,2,0,1:T(8,128)(2,1)S(1)}, bf16[16,8,16,128]{3,2,0,1:T(8,128)(2,1)}, u32[]{:S(2)}) copy-start(bf16[16,8,16,128]{3,2,0,1:T(8,128)(2,1)} %copy-done.2) | copy-start | bytes 1572868
  87.6 0.7 copy-start.4
  114.7 72.4 %all-to-all-start.2 = ((bf16[8,256,128]{2,0,1:T(8,128)(2,1)}), bf16[8,256,128]{2,0,1:T(8,128)(2,1)S(1)}, u32[]{:S(2)}, u32[]{:S(2)}) async-start(bf16[8,256,128]{2,0,1:T(8,128)(2,1)} %copy.43), calls=%async_computation.3 | async-start | bytes 1048576 | tf_op jit(solution)/shard_map/all_to_all | solution.py:122
  361.9 25.5 %all-to-all-start.3 = ((bf16[16,2,1024]{2,1,0:T(2,128)(2,1)}), bf16[16,2,1024]{2,1,0:T(2,128)(2,1)S(1)}, u32[]{:S(2)}, u32[]{:S(2)}) async-start(bf16[16,2,1024]{2,1,0:T(2,128)(2,1)} %reshape.73), calls=%async_computation.4 | async-start | bytes 131072 | tf_op jit(solution)/shard_map/all_to_all | solution.py:125
Sparse Core Ops, SparseCore 0:
  55.8 128.9 all-reduce.1
  189.3 105.4 reduce-scatter.1
  297.9 60.8 all-gather.1
where the time goes:
time: 396 us; the launch traced here: 395 us
  waiting for transfers between devices  242 us (61%)
  blocking collectives  93.4 us (24%)
  starting transfers between devices  18.2 us (5%)
  matrix products  15 us (4%)
  between operations  14 us (4%)
  local copies, waits for them, and re-layouts  10.2 us (3%)
    reduce_scatter x1, waiting for transfers between devices, body(): lax.psum_scatter(jnp.dot(tokens, key_value_weight, preferred_element_type...  106 us
    psum x1, waiting for transfers between devices, body(): low_all = lax.psum(low_part.astype(jnp.bfloat16), ('pipe', 'tensor'))  63.9 us
    all_gather x1, waiting for transfers between devices, body(): lax.all_gather(cotangent, ('pipe', 'tensor'), axis=0, tiled=True)  62.4 us
    all_to_all x1, blocking collectives, body(): lax.all_to_all(a_send, 'dp', split_axis=0, concat_axis=1, tiled=True)  44.1 us
    all_gather x1, blocking collectives, body(): lax.all_gather(grad_rows, ('pipe', 'tensor'), axis=0, tiled=True)  24.9 us
    all_to_all x1, blocking collectives, body(): lax.all_to_all(b_send, 'dp', split_axis=0, concat_axis=1, tiled=True)  24.5 us
    all_to_all x1, starting transfers between devices, body(): lax.all_to_all(grad_b_part.astype(jnp.bfloat16), 'dp', split_axis=1, conc...  12.3 us
    all_to_all x1, waiting for transfers between devices, body(): lax.all_to_all(grad_b_part.astype(jnp.bfloat16), 'dp', split_axis=1, conc...  8.89 us
  transfers between devices with their start and end apart: 5, of which 4 were waited for; matrix products, arithmetic and copies ran while one was open for 5% of the time, Pallas kernels for 0%

commit v1 on v0

--- a/solution.py
+++ b/solution.py
@@ -54,7 +54,13 @@
     low_part = jnp.einsum(
         "bif,bfr->bir", tok_blocks, down_blocks, preferred_element_type=jnp.float32
     ).reshape(tok_dev, 2 * ADAPTER_RANK)
-    low_all = lax.psum(low_part.astype(jnp.bfloat16), ("pipe", "tensor"))
+
+    def lead_core_for(vector, axis_key, dev_axis):
+        for hop_no in (axis_key, dev_axis):
+            vector = jax.lax.psum(vector, hop_no)
+        return vector
+
+    low_all = lead_core_for(low_part.astype(jnp.bfloat16), "pipe", "tensor")
     base_out = lax.psum_scatter(
         jnp.dot(tokens, key_value_weight, preferred_element_type=jnp.float32).astype(jnp.bfloat16),
         ("pipe", "tensor"),

time: 396 us -> 322 us (0.81)
  waiting for transfers between devices: 242 us -> 163 us
  blocking collectives: 93.4 us -> 97.5 us
    reduce_scatter x1, waiting for transfers between devices: 106 us -> 12.4 us  [body(): lax.psum_scatter(jnp.dot(tokens, key_value_weight, preferred_element_type...]
    all_to_all x1, waiting for transfers between devices: 0.01 us -> 11.7 us  [body(): lax.all_to_all(grad_a_part.astype(jnp.bfloat16), 'dp', split_axis=1, conc...]
    all_to_all x1, blocking collectives: 24.5 us -> 29 us  [body(): lax.all_to_all(b_send, 'dp', split_axis=0, concat_axis=1, tiled=True)]
    psum x1 -> x2, waiting for transfers between devices: 63.9 us -> 67 us  [lead_core_for(): vector = jax.lax.psum(vector, hop_no)]
  transfers between devices with their start and end apart: 5 -> 6, of which waited for: 4 -> 6; matrix products, arithmetic and copies ran while one was open for 5% -> 6% of each run, Pallas kernels for 0% -> 0%
where the time goes in v1:
time: 322 us
  waiting for transfers between devices  163 us (51%)
  blocking collectives  97.5 us (30%)
  starting transfers between devices  17.7 us (5%)
  between operations  15.8 us (5%)
  matrix products  15 us (5%)
  local copies, waits for them, and re-layouts  10.2 us (3%)
    psum x2, waiting for transfers between devices, lead_core_for(): vector = jax.lax.psum(vector, hop_no)  67 us
    all_gather x1, waiting for transfers between devices, body(): lax.all_gather(cotangent, ('pipe', 'tensor'), axis=0, tiled=True)  62.3 us
    all_to_all x1, blocking collectives, body(): lax.all_to_all(a_send, 'dp', split_axis=0, concat_axis=1, tiled=True)  44.1 us
    all_to_all x1, blocking collectives, body(): lax.all_to_all(b_send, 'dp', split_axis=0, concat_axis=1, tiled=True)  29 us
    all_gather x1, blocking collectives, body(): lax.all_gather(grad_rows, ('pipe', 'tensor'), axis=0, tiled=True)  24.4 us
    reduce_scatter x1, waiting for transfers between devices, body(): lax.psum_scatter(jnp.dot(tokens, key_value_weight, preferred_element_type...  12.4 us
    all_to_all x1, starting transfers between devices, body(): lax.all_to_all(grad_b_part.astype(jnp.bfloat16), 'dp', split_axis=1, conc...  12.3 us
    all_to_all x1, waiting for transfers between devices, body(): lax.all_to_all(grad_a_part.astype(jnp.bfloat16), 'dp', split_axis=1, conc...  11.7 us
  transfers between devices with their start and end apart: 6, of which 6 were waited for; matrix products, arithmetic and copies ran while one was open for 6% of the time, Pallas kernels for 0%

profile of v1, /device:TPU:2, one launch (start us, length us, event | category | flops | bytes accessed | tf_op | source)
XLA Modules:
  0.0 321.5 jit_solution(1179407160290872442)
XLA Ops:
  8.1 0.9 select_reduce_fusion
  9.0 1.3 fusion.2
  10.3 0.1 copy.60
  10.4 44.1 %all_to_all.57 = bf16[128,16,128]{2,1,0:T(8,128)(2,1)S(1)} all-to-all(bf16[128,16,128]{2,1,0:T(8,128)(2,1)S(1)} %bitcast.78), channel_id=1, replica_groups=mesh['dp'=16,'pipe'=4,'tensor'=8] {'dp'}, dimensions={0} | all-to-all | bytes 1048576 | tf_op jit(solution)/shard_map/all_to_all | solution.py:49
  54.5 0.8 copy-done.2
  55.3 0.3 convolution_convert_fusion.4
  55.6 0.9 copy.41
  56.5 52.0 %all-reduce.3.cloned.1.call-done = bf16[1024,128]{0,1:T(8,128)(2,1)} async-done(((bf16[1024,128]{0,1:T(8,128)(2,1)}), bf16[1024,128]{0,1:T(8,128)(2,1)}) %all-reduce.3.cloned.1.call-update) | async-done | bytes 262160 | tf_op jit(solution)/shard_map/psum | solution.py:60
  108.6 3.2 %convolution_convert_fusion.1 = bf16[1024,2048]{1,0:T(8,128)(2,1)} fusion(bf16[1024,256]{1,0:T(8,128)(2,1)S(1)} %copy-done.1, bf16[256,2048]{1,0:T(8,128)(2,1)S(1)} %copy-done), kind=kOutput, calls=%fused_computation.1 | convolution fusion | flops 1075838976 | bytes 5767168 | tf_op jit(solution)/shard_map/dot_general | solution.py:65
  111.9 0.5 all-gather.2.cloned.1.call-update
  112.5 0.1 reshape.62
  112.6 2.4 copy.61
  115.0 0.2 dynamic-slice_reduce_fusion
  115.2 0.4 convolution_convert_fusion
  115.6 0.2 reshape.64
  115.8 29.0 %all_to_all.58 = bf16[16,4,2048]{2,1,0:T(4,128)(2,1)S(1)} all-to-all(bf16[16,4,2048]{2,1,0:T(4,128)(2,1)S(1)} %reshape.64), channel_id=1, replica_groups=mesh['dp'=16,'pipe'=4,'tensor'=8] {'dp'}, dimensions={0} | all-to-all | bytes 524288 | tf_op jit(solution)/shard_map/all_to_all | solution.py:50
  144.8 0.1 squeeze.5
  144.9 0.1 fusion.3
  145.0 0.2 fusion.4
  145.2 0.4 copy-done.4
  145.6 0.1 pad_maximum_fusion
  145.7 24.4 %all_gather.7 = bf16[1024,128]{1,0:T(8,128)(2,1)S(1)} all-gather(bf16[32,128]{1,0:T(8,128)(2,1)S(1)} %pad_maximum_fusion), channel_id=1, replica_groups=mesh['dp'=16,'pipe'=4,'tensor'=8] {'pipe','tensor'}, dimensions={0}, use_global_device_ids=true | all-gather | bytes 270336 | tf_op jit(solution)/shard_map/all_gather | solution.py:104
  170.1 0.3 fusion.1
  170.4 1.1 copy.43
  171.5 5.2 %all-to-all-start.2 = ((bf16[8,256,128]{2,0,1:T(8,128)(2,1)}), bf16[8,256,128]{2,0,1:T(8,128)(2,1)S(1)}, u32[]{:S(2)}, u32[]{:S(2)}) async-start(bf16[8,256,128]{2,0,1:T(8,128)(2,1)} %copy.43), calls=%async_computation.3 | async-start | bytes 1048576 | tf_op jit(solution)/shard_map/all_to_all | solution.py:128
  176.8 0.3 fusion.30
  177.1 15.0 %all-reduce.5.cloned.1.call-done = bf16[1024,128]{0,1:T(8,128)(2,1)} async-done(((bf16[1024,128]{0,1:T(8,128)(2,1)}), bf16[1024,128]{0,1:T(8,128)(2,1)}) %all-reduce.5.cloned.1.call-update) | async-done | bytes 262160 | tf_op jit(solution)/shard_map/psum | solution.py:60
  192.1 1.2 fusion.14
  193.2 1.2 fusion.11
  194.4 11.7 %all-to-all-done.2 = bf16[8,256,128]{2,0,1:T(8,128)(2,1)S(1)} async-done(((bf16[8,256,128]{2,0,1:T(8,128)(2,1)}), bf16[8,256,128]{2,0,1:T(8,128)(2,1)S(1)}, u32[]{:S(2)}, u32[]{:S(2)}) %all-to-all-start.2) | async-done | bytes 524320 | tf_op jit(solution)/shard_map/all_to_all | solution.py:128
  206.1 0.3 copy.46
  206.4 0.3 fusion.21
  206.7 1.3 copy.53
  208.0 12.4 %reduce-scatter.2.cloned.1.call-done = bf16[32,2048]{1,0:T(8,128)(2,1)} async-done(((bf16[1024,2048]{1,0:T(8,128)(2,1)}), bf16[32,2048]{1,0:T(8,128)(2,1)}) %reduce-scatter.2.cloned.1.call-update) | async-done | bytes 131088 | tf_op jit(solution)/shard_map/reduce_scatter | solution.py:64
  220.4 1.6 fusion.7
  222.0 62.3 %all-gather.2.cloned.1.call-done = bf16[1024,2048]{1,0:T(8,128)(2,1)} async-done(((bf16[32,2048]{1,0:T(8,128)(2,1)}), bf16[1024,2048]{1,0:T(8,128)(2,1)}) %all-gather.2.cloned.1.call-update) | async-done | bytes 4194320 | tf_op jit(solution)/shard_map/all_gather | solution.py:103
  284.2 1.1 constant_dynamic-slice_fusion
  285.3 1.1 convolution_convert_fusion.5
  286.5 0.1 copy.73
  286.6 0.8 reshape.73
  287.3 12.3 %all-to-all-start.3 = ((bf16[16,2,1024]{2,1,0:T(2,128)(2,1)}), bf16[16,2,1024]{2,1,0:T(2,128)(2,1)S(1)}, u32[]{:S(2)}, u32[]{:S(2)}) async-start(bf16[16,2,1024]{2,1,0:T(2,128)(2,1)} %reshape.73), calls=%async_computation.4 | async-start | bytes 131072 | tf_op jit(solution)/shard_map/all_to_all | solution.py:131
  299.6 4.3 %fusion = bf16[1024,256]{1,0:T(8,128)(2,1)} fusion(f32[1024,256]{1,0:T(8,128)S(1)} %bitcast.81, bf16[1024,2048]{1,0:T(8,128)(2,1)} %all-gather.2.cloned.1.call-done, bf16[256,2048]{1,0:T(8,128)(2,1)S(1)} %copy-done), kind=kOutput, calls=%fused_computation.4 | convolution fusion | flops 1074266112 | bytes 6815744 | tf_op jit(solution)/shard_map/dot_general | solution.py:107
  303.9 8.9 %all-to-all-done.3 = bf16[16,2,1024]{2,1,0:T(2,128)(2,1)S(1)} async-done(((bf16[16,2,1024]{2,1,0:T(2,128)(2,1)}), bf16[16,2,1024]{2,1,0:T(2,128)(2,1)S(1)}, u32[]{:S(2)}, u32[]{:S(2)}) %all-to-all-start.3) | async-done | bytes 65568 | tf_op jit(solution)/shard_map/all_to_all | solution.py:131
  312.8 0.1 reshape.74
  312.9 0.1 copy.72
  313.0 0.1 reshape.70
  313.1 0.1 copy.52
  313.2 0.8 fusion.19
  (18 shorter events, 0.3 us)
Async XLA Ops:
  8.0 100.6 %copy-start = (bf16[256,2048]{1,0:T(8,128)(2,1)S(1)}, bf16[256,2048]{1,0:T(8,128)(2,1)}, u32[]{:S(2)}) copy-start(bf16[256,2048]{1,0:T(8,128)(2,1)} %param.8) | copy-start | bytes 3145732
  8.0 47.3 %copy-start.1 = (bf16[1024,256]{1,0:T(8,128)(2,1)S(1)}, bf16[1024,256]{1,0:T(8,128)(2,1)}, u32[]{:S(2)}) copy-start(bf16[1024,256]{1,0:T(8,128)(2,1)} %param.7) | copy-start | bytes 1572868
  8.0 100.5 %all-reduce.3.cloned.1.call-start = ((), (), s32[]{:S(2)}) async-start(), calls=%async_computation.6 | async-start | bytes 524288 | tf_op jit(solution)/shard_map/psum | solution.py:60
  54.5 0.8 copy-start.2
  56.5 135.6 %all-reduce.5.cloned.1.call-start = ((), (), s32[]{:S(2)}) async-start(), calls=%async_computation.7 | async-start | bytes 524288 | tf_op jit(solution)/shard_map/psum | solution.py:60
  108.5 111.9 %reduce-scatter.2.cloned.1.call-start = ((), (), s32[]{:S(2)}) async-start(), calls=%async_computation.5 | async-start | bytes 4325376 | tf_op jit(solution)/shard_map/reduce_scatter | solution.py:64
  111.9 33.0 %copy-start.5 = (bf16[32,2048]{1,0:T(8,128)(2,1)S(1)}, bf16[32,2048]{1,0:T(8,128)(2,1)}, u32[]{:S(2)}) copy-start(bf16[32,2048]{1,0:T(8,128)(2,1)} %param.13) | copy-start | bytes 393220
  111.9 172.4 %all-gather.2.cloned.1.call-start = ((), (), s32[]{:S(2)}) async-start(), calls=%async_computation.8 | async-start | bytes 4325376 | tf_op jit(solution)/shard_map/all_gather | solution.py:103
  115.6 61.2 %copy-start.3 = (bf16[16,8,16,128]{3,2,0,1:T(8,128)(2,1)S(1)}, bf16[16,8,16,128]{3,2,0,1:T(8,128)(2,1)}, u32[]{:S(2)}) copy-start(bf16[16,8,16,128]{3,2,0,1:T(8,128)(2,1)} %copy-done.2) | copy-start | bytes 1572868
  144.9 0.7 copy-start.4
  171.5 34.6 %all-to-all-start.2 = ((bf16[8,256,128]{2,0,1:T(8,128)(2,1)}), bf16[8,256,128]{2,0,1:T(8,128)(2,1)S(1)}, u32[]{:S(2)}, u32[]{:S(2)}) async-start(bf16[8,256,128]{2,0,1:T(8,128)(2,1)} %copy.43), calls=%async_computation.3 | async-start | bytes 1048576 | tf_op jit(solution)/shard_map/all_to_all | solution.py:128
  287.3 25.5 %all-to-all-start.3 = ((bf16[16,2,1024]{2,1,0:T(2,128)(2,1)}), bf16[16,2,1024]{2,1,0:T(2,128)(2,1)S(1)}, u32[]{:S(2)}, u32[]{:S(2)}) async-start(bf16[16,2,1024]{2,1,0:T(2,128)(2,1)} %reshape.73), calls=%async_computation.4 | async-start | bytes 131072 | tf_op jit(solution)/shard_map/all_to_all | solution.py:131
Sparse Core Ops, SparseCore 0:
  56.6 51.8 all-reduce.2
  110.8 81.1 all-reduce.4
Sparse Core Ops, SparseCore 1:
  113.5 106.8 reduce-scatter.1
  223.4 60.8 all-gather.1
